TPU v7x, 512 devices: a whole 4x4x16 slice. The times are simulated.
512 devices in a mesh: mp: 8 (over z_lo, core), feat: 64 (over x, z_hi, y).
Axes of the slice: x: 4, y: 4, z: 16 (z_hi: 4, z_lo: 4; z = z_hi * 4 + z_lo), core: 2. Of those that a mesh axis runs over, the one named last changes fastest.
Arguments:
- target_ids: int32 [16], replicated, may hold values from 0 to 127999
- target_pos: int32 [16], replicated, may hold values from 24 to 47
- unembed: bfloat16 [128000, 2304], P(('mp', 'feat')), may hold values from -6 to 6
- attn_weights: float32 [8, 16, 48, 48], P('mp'), may hold values from 0.02 to 1
- inv_rms: float32 [16, 48], replicated, may hold values from 0.5 to 2
- norm_gain: float32 [2304], replicated, may hold values from 0.1 to 1.9
- w_value: bfloat16 [4, 2304, 256], P(None, 'mp'), may hold values from -0.125 to 0.125
- w_out: bfloat16 [8, 256, 2304], P('mp'), may hold values from -0.375 to 0.375
- decoder: bfloat16 [2, 98304, 2304], P(None, ('mp', 'feat')), may hold values from -0.125 to 0.125
- activation: bfloat16 [16, 48, 98304], P(None, None, ('mp', 'feat')), may hold values from 0.5 to 4
- active: int32 [16, 48, 98304], P(None, None, ('mp', 'feat')), may hold values 0 or 1
Outputs:
- attribution: float32 [16, 48, 98304], P(None, None, ('mp', 'feat'))
All inputs are finite; a program needn't handle non-finite values. No bound on the sum of `active` on one device may be relied on, other than what follows from the above.
Results may differ from a plain program's by a relative error of at most 0.0035.
Values may be sent and summed in bfloat16 or wider, within the bound.
No kernel may reach another device: no remote copies, remote signals or barrier semaphores. Data moves between devices by JAX's collectives and lax.ppermute only.
A program may use at most 64 MiB of HBM per device.

v0:
```python
import jax
import jax.numpy as jnp
from jax import lax
from jax.sharding import PartitionSpec as P


def on_device(
    target_ids,
    target_pos,
    unembed,
    attn_weights,
    inv_rms,
    norm_gain,
    w_value,
    w_out,
    decoder,
    activation,
    active,
):
    vocab_rows = unembed.shape[0]
    model_width = unembed.shape[1]
    targets = target_ids.shape[0]
    positions = inv_rms.shape[1]
    local_heads = w_out.shape[0]
    kv_heads = w_value.shape[0]
    column_count = w_value.shape[1]
    row_count = targets * positions
    own_rows = row_count // lax.axis_size("feat")
    device_rank = lax.axis_index("mp") * lax.axis_size("feat") + lax.axis_index("feat")
    first_row = device_rank * vocab_rows
    picker = (
        target_ids[:, None] == first_row + jnp.arange(vocab_rows, dtype=jnp.int32)[None, :]
    ).astype(jnp.bfloat16)
    direction = lax.psum(
        jnp.dot(picker, unembed, preferred_element_type=jnp.float32), ("mp", "feat")
    )
    placing = (jnp.arange(positions, dtype=jnp.int32)[None, :] == target_pos[:, None]).astype(
        jnp.float32
    )
    upper = (placing[:, :, None] * direction[:, None, :]).reshape(row_count, model_width)
    lowered_top = upper.astype(jnp.bfloat16)
    row_start = lax.axis_index("feat") * own_rows
    column_start = lax.axis_index("mp") * column_count
    index_pos = jnp.arange(positions, dtype=jnp.int32)
    causal = (index_pos[:, None] >= index_pos[None, :]).astype(jnp.float32)
    weights = attn_weights * causal
    pattern = weights / jnp.sum(weights, axis=-1, keepdims=True)
    flipped = jnp.swapaxes(pattern, 2, 3).reshape(local_heads, row_count, positions)
    own_pattern = lax.dynamic_slice_in_dim(flipped, row_start, own_rows, 1)
    row_group = (row_start + jnp.arange(own_rows, dtype=jnp.int32)) // positions
    group_pick = (row_group[:, None] == jnp.arange(targets, dtype=jnp.int32)[None, :]).astype(
        jnp.float32
    )
    block_pattern = (own_pattern[:, :, None, :] * group_pick[None, :, :, None]).reshape(
        local_heads, own_rows, row_count
    )
    mixed = jnp.einsum(
        "hrq,qd->hrd",
        block_pattern,
        lowered_top.astype(jnp.float32),
        precision=lax.Precision.HIGHEST,
    ).astype(jnp.bfloat16)
    spread = jnp.einsum("hrd,hkd->hrk", mixed, w_out, preferred_element_type=jnp.float32).astype(
        jnp.bfloat16
    )
    all_spread = lax.all_gather(spread, "mp", axis=0, tiled=True)
    group_size = local_heads * lax.axis_size("mp") // kv_heads
    value_heads = jnp.repeat(w_value, group_size, axis=0)
    heads_sum = jnp.einsum(
        "hrk,hck->rc", all_spread, value_heads, preferred_element_type=jnp.float32
    )
    upper_rows = lax.dynamic_slice_in_dim(upper, row_start, own_rows, 0)
    upper_block = lax.dynamic_slice_in_dim(upper_rows, column_start, column_count, 1)
    scale_rows = lax.dynamic_slice_in_dim(inv_rms.reshape(row_count, 1), row_start, own_rows, 0)
    gain_columns = lax.dynamic_slice_in_dim(norm_gain, column_start, column_count, 0)
    below_block = upper_block + scale_rows * gain_columns[None, :] * heads_sum
    lowered_block = below_block.astype(jnp.bfloat16)
    top_scores = jnp.einsum(
        "rd,fd->rf", lowered_top, decoder[1], preferred_element_type=jnp.float32
    )
    tall_block = lax.all_gather(lowered_block, "feat", axis=0, tiled=True)
    lowered_bottom = lax.all_gather(tall_block, "mp", axis=1, tiled=True)
    bottom_scores = jnp.einsum(
        "rd,fd->rf", lowered_bottom, decoder[0], preferred_element_type=jnp.float32
    )
    scores = bottom_scores + top_scores
    feature_count = decoder.shape[1]
    attribution = (
        activation.astype(jnp.float32).reshape(row_count, feature_count)
        * active.reshape(row_count, feature_count).astype(jnp.float32)
        * scores
    )
    return attribution.reshape(targets, positions, feature_count)


def solution(mesh):
    in_specs = (
        P(),
        P(),
        P(("mp", "feat"), None),
        P("mp", None, None, None),
        P(),
        P(),
        P(None, "mp", None),
        P("mp", None, None),
        P(None, ("mp", "feat"), None),
        P(None, None, ("mp", "feat")),
        P(None, None, ("mp", "feat")),
    )
    out_specs = P(None, None, ("mp", "feat"))
    return jax.shard_map(
        on_device, mesh=mesh, in_specs=in_specs, out_specs=out_specs, check_vma=False
    )
```

profile of v0, /device:TPU:2, one launch (start us, length us, event | category | flops | bytes accessed | tf_op | source)
XLA Modules:
  0.0 761.0 jit_solution(12552327615252992566)
XLA Ops:
  6.5 0.0 copy-start
  6.5 0.0 copy-start.7
  6.5 0.0 copy-start.6
  6.5 0.0 all-reduce.2.cloned.1.call-start
  6.6 1.2 copy-done
  7.8 0.0 copy-start.1
  7.8 1.7 fusion.23
  9.5 0.0 all-reduce.2.cloned.1.call-update
  9.6 0.0 all-gather.5.cloned.1.call-start
  9.7 1.2 multiply_reduce_fusion
  10.8 1.2 divide_bitcast_fusion
  12.0 0.1 copy.21
  12.1 0.2 reshape.175
  12.3 0.1 constant_dynamic-slice_fusion
  12.4 0.1 copy.22
  12.5 0.0 copy-done.7
  12.5 0.1 fusion.27
  12.6 0.1 reshape.179
  12.7 0.0 copy-done.6
  12.7 0.1 reshape.174
  12.7 0.8 dynamic_slice.15
  13.5 0.1 dynamic-slice
  13.6 0.1 dynamic-slice_bitcast_fusion
  13.7 450.9 %all-reduce.2.cloned.1.call-done = f32[16,2304]{1,0:T(8,128)} async-done(((f32[16,2304]{1,0:T(8,128)}), f32[16,2304]{1,0:T(8,128)}) %all-reduce.2.cloned.1.call-update) | async-done | bytes 147472 | tf_op jit(solution)/shard_map/psum | solution.py:34
  464.6 0.0 copy-start.4
  464.6 2.9 fusion
  467.5 0.0 copy-done.1
  467.5 0.4 fusion.11
  467.8 14.0 %all-gather.1 = bf16[8,12,256]{2,1,0:T(8,128)(2,1)S(1)} all-gather(bf16[1,12,256]{2,1,0:T(8,128)(2,1)S(1)} %fusion.11), channel_id=2, replica_groups=mesh['mp'=8,'feat'=64] {'mp'}, dimensions={0}, use_global_device_ids=true | all-gather | bytes 55296 | tf_op jit(solution)/shard_map/all_gather | solution.py:66
  481.9 0.0 copy-done.4
  481.9 0.0 copy-start.3
  481.9 0.5 mul.102
  482.4 0.0 copy-start.2
  482.4 0.5 copy-done.3
  482.9 0.1 broadcast_in_dim.2
  483.0 0.4 fusion.7
  483.5 202.2 %all-gather.2 = bf16[64,12,288]{2,1,0:T(8,128)(2,1)S(1)} all-gather(bf16[1,12,288]{2,1,0:T(8,128)(2,1)S(1)} %fusion.7), channel_id=1, replica_groups=mesh['mp'=8,'feat'=64] {'feat'}, dimensions={0}, use_global_device_ids=true | all-gather | bytes 449280 | tf_op jit(solution)/shard_map/all_gather | solution.py:81
  685.7 0.3 reshape.184
  686.0 1.0 copy.23
  687.0 0.0 all-gather.5.cloned.1.call-update
  687.0 0.0 copy-done.2
  687.0 1.1 convert_multiply_fusion
  688.1 0.2 copy.24
  688.4 0.0 copy-start.5
  688.4 0.5 multiply_convert_fusion
  688.9 0.9 copy-done.5
  689.9 1.3 fusion.14
  691.2 58.7 %all-gather.5.cloned.1.call-done = bf16[768,2304]{0,1:T(8,128)(2,1)} async-done(((bf16[768,288]{0,1:T(8,128)(2,1)}), bf16[768,2304]{0,1:T(8,128)(2,1)}) %all-gather.5.cloned.1.call-update) | async-done | bytes 3538960 | tf_op jit(solution)/shard_map/all_gather | solution.py:82
  749.9 3.1 fusion.1
  753.0 1.1 copy.25
  (4 shorter events, 0.0 us)
Async XLA Ops:
  6.5 1.3 copy-start
  6.5 6.0 copy-start.7
  6.5 6.1 copy-start.6
  6.5 458.1 %all-reduce.2.cloned.1.call-start = ((), (), s32[]{:S(2)}) async-start(), calls=%async_computation | async-start | bytes 294912 | tf_op jit(solution)/shard_map/psum | solution.py:34
  7.8 459.7 %copy-start.1 = (bf16[1,256,2304]{2,1,0:T(8,128)(2,1)S(1)}, bf16[1,256,2304]{2,1,0:T(8,128)(2,1)}, u32[]{:S(2)}) copy-start(bf16[1,256,2304]{2,1,0:T(8,128)(2,1)} %param.18) | copy-start | bytes 3538948
  9.6 740.3 %all-gather.5.cloned.1.call-start = ((), (), s32[]{:S(2)}) async-start(), calls=%async_computation.1 | async-start | bytes 3981312 | tf_op jit(solution)/shard_map/all_gather | solution.py:82
  464.6 17.3 %copy-start.4 = (f32[16,2304]{1,0:T(8,128)S(1)}, f32[16,2304]{1,0:T(8,128)}, u32[]{:S(2)}) copy-start(f32[16,2304]{1,0:T(8,128)} %all-reduce.2.cloned.1.call-done) | copy-start | bytes 442372
  481.9 1.1 copy-start.3
  482.4 204.6 %copy-start.2 = (s32[16,48,192]{2,1,0:T(8,128)S(1)}, s32[16,48,192]{2,1,0:T(8,128)}, u32[]{:S(2)}) copy-start(s32[16,48,192]{2,1,0:T(8,128)} %param.21) | copy-start | bytes 1769476
  688.4 1.5 copy-start.5
Sparse Core Ops, SparseCore 0:
  12.8 451.7 all-reduce.1
  687.1 62.7 all-gather.4
where the time goes:
time: 761 us
  waiting for transfers between devices  510 us (67%)
  blocking collectives  216 us (28%)
  between operations  13.6 us (2%)
  matrix products  9.86 us (1%)
    psum x1, waiting for transfers between devices, on_device(): lax.psum(jnp.dot(picker, unembed, preferred_element_type=jnp.float32), ('...  451 us
    all_gather x1, blocking collectives, on_device(): tall_block = lax.all_gather(lowered_block, 'feat', axis=0, tiled=True)  202 us
    all_gather x1, waiting for transfers between devices, on_device(): lowered_bottom = lax.all_gather(tall_block, 'mp', axis=1, tiled=True)  58.7 us
  transfers between devices with their start and end apart: 2, of which 2 were waited for; matrix products, arithmetic and copies ran while one was open for 1% of the time, Pallas kernels for 0%

commit v1 on v0

--- a/solution.py
+++ b/solution.py
@@ -32,7 +32,7 @@
         target_ids[:, None] == first_row + jnp.arange(vocab_rows, dtype=jnp.int32)[None, :]
     ).astype(jnp.bfloat16)
     direction = lax.psum(
-        jnp.dot(picker, unembed, preferred_element_type=jnp.float32), ("mp", "feat")
+        lax.psum(jnp.dot(picker, unembed, preferred_element_type=jnp.float32), "mp"), "feat"
     )
     placing = (jnp.arange(positions, dtype=jnp.int32)[None, :] == target_pos[:, None]).astype(
         jnp.float32

time: 761 us -> 1160 us (1.52)
  waiting for transfers between devices: 510 us -> 904 us
    psum x1 -> x2, waiting for transfers between devices: 451 us -> 820 us  [the longest x1 740 us: on_device(): lax.psum(lax.psum(jnp.dot(picker, unembed, preferred_element_type=jnp.flo...]
    all_gather x1, waiting for transfers between devices: 58.7 us -> 84.1 us  [on_device(): lowered_bottom = lax.all_gather(tall_block, 'mp', axis=1, tiled=True)]
  transfers between devices with their start and end apart: 2 -> 3, of which waited for: 2 -> 3; matrix products, arithmetic and copies ran while one was open for 1% -> 1% of each run, Pallas kernels for 0% -> 0%
where the time goes in v1:
time: 1160 us
  waiting for transfers between devices  904 us (78%)
  blocking collectives  218 us (19%)
  between operations  13.3 us (1%)
    psum x1, waiting for transfers between devices, on_device(): lax.psum(lax.psum(jnp.dot(picker, unembed, preferred_element_type=jnp.flo...  740 us
    all_gather x1, blocking collectives, on_device(): tall_block = lax.all_gather(lowered_block, 'feat', axis=0, tiled=True)  204 us
    all_gather x1, waiting for transfers between devices, on_device(): lowered_bottom = lax.all_gather(tall_block, 'mp', axis=1, tiled=True)  84.1 us
    psum x1, waiting for transfers between devices, on_device(): lax.psum(jnp.dot(picker, unembed, preferred_element_type=jnp.float32), 'mp')  80 us
  transfers between devices with their start and end apart: 3, of which 3 were waited for; matrix products, arithmetic and copies ran while one was open for 1% of the time, Pallas kernels for 0%

profile of v1, /device:TPU:2, one launch (start us, length us, event | category | flops | bytes accessed | tf_op | source)
XLA Modules:
  0.0 1157.5 jit_solution(6221271685507907421)
XLA Ops:
  6.5 0.0 copy-start
  6.5 0.0 copy-start.7
  6.5 0.0 copy-start.6
  6.5 0.0 all-reduce.3.cloned.1.call-start
  6.6 1.2 copy-done
  7.8 1.6 fusion.23
  9.4 0.0 copy-start.1
  9.4 0.0 all-reduce.3.cloned.1.call-update
  9.5 0.0 all-reduce.5.cloned.1.call-start
  9.6 1.2 multiply_reduce_fusion
  10.8 1.2 divide_bitcast_fusion
  12.0 0.1 copy.21
  12.1 0.2 reshape.175
  12.3 0.0 copy-done.7
  12.3 0.1 fusion.27
  12.4 80.0 %all-reduce.3.cloned.1.call-done = f32[16,2304]{1,0:T(8,128)} async-done(((f32[16,2304]{1,0:T(8,128)}), f32[16,2304]{1,0:T(8,128)}) %all-reduce.3.cloned.1.call-update) | async-done | bytes 147472 | tf_op jit(solution)/shard_map/psum | solution.py:35
  92.4 0.0 all-reduce.5.cloned.1.call-update
  92.5 0.0 all-gather.5.cloned.1.call-start
  92.5 0.1 constant_dynamic-slice_fusion
  92.6 0.1 copy.22
  92.7 0.1 reshape.179
  92.8 0.0 copy-done.6
  92.8 0.1 reshape.174
  92.9 0.8 dynamic_slice.15
  93.6 0.1 dynamic-slice
  93.7 0.1 dynamic-slice_bitcast_fusion
  93.8 740.2 %all-reduce.5.cloned.1.call-done = f32[16,2304]{1,0:T(8,128)} async-done(((f32[16,2304]{1,0:T(8,128)}), f32[16,2304]{1,0:T(8,128)}) %all-reduce.5.cloned.1.call-update) | async-done | bytes 147472 | tf_op jit(solution)/shard_map/psum | solution.py:34
  834.0 0.0 copy-start.4
  834.0 2.9 fusion
  836.9 0.0 copy-done.1
  836.9 0.4 fusion.11
  837.3 14.0 %all-gather.1 = bf16[8,12,256]{2,1,0:T(8,128)(2,1)S(1)} all-gather(bf16[1,12,256]{2,1,0:T(8,128)(2,1)S(1)} %fusion.11), channel_id=2, replica_groups=mesh['mp'=8,'feat'=64] {'mp'}, dimensions={0}, use_global_device_ids=true | all-gather | bytes 55296 | tf_op jit(solution)/shard_map/all_gather | solution.py:66
  851.3 0.0 copy-done.4
  851.3 0.0 copy-start.3
  851.3 0.5 mul.102
  851.8 0.0 copy-start.2
  851.9 0.5 copy-done.3
  852.4 0.1 broadcast_in_dim.2
  852.4 0.4 fusion.7
  852.9 204.3 %all-gather.2 = bf16[64,12,288]{2,1,0:T(8,128)(2,1)S(1)} all-gather(bf16[1,12,288]{2,1,0:T(8,128)(2,1)S(1)} %fusion.7), channel_id=1, replica_groups=mesh['mp'=8,'feat'=64] {'feat'}, dimensions={0}, use_global_device_ids=true | all-gather | bytes 449280 | tf_op jit(solution)/shard_map/all_gather | solution.py:81
  1057.2 0.3 reshape.184
  1057.5 1.0 copy.23
  1058.5 0.0 all-gather.5.cloned.1.call-update
  1058.5 0.0 copy-done.2
  1058.5 1.1 convert_multiply_fusion
  1059.6 0.2 copy.24
  1059.8 0.0 copy-start.5
  1059.9 0.5 multiply_convert_fusion
  1060.4 0.9 copy-done.5
  1061.3 1.3 fusion.14
  1062.6 84.1 %all-gather.5.cloned.1.call-done = bf16[768,2304]{0,1:T(8,128)(2,1)} async-done(((bf16[768,288]{0,1:T(8,128)(2,1)}), bf16[768,2304]{0,1:T(8,128)(2,1)}) %all-gather.5.cloned.1.call-update) | async-done | bytes 3538960 | tf_op jit(solution)/shard_map/all_gather | solution.py:82
  1146.7 3.1 fusion.1
  1149.8 1.1 copy.25
  (4 shorter events, 0.0 us)
Async XLA Ops:
  6.5 1.3 copy-start
  6.5 5.8 copy-start.7
  6.5 86.2 %copy-start.6 = (f32[16,48]{1,0:T(8,128)S(1)}, f32[16,48]{1,0:T(8,128)}, u32[]{:S(2)}) copy-start(f32[16,48]{1,0:T(8,128)} %param.15) | copy-start | bytes 9220
  6.5 85.9 %all-reduce.3.cloned.1.call-start = ((), (), s32[]{:S(2)}) async-start(), calls=%async_computation | async-start | bytes 294912 | tf_op jit(solution)/shard_map/psum | solution.py:35
  9.4 827.4 %copy-start.1 = (bf16[1,256,2304]{2,1,0:T(8,128)(2,1)S(1)}, bf16[1,256,2304]{2,1,0:T(8,128)(2,1)}, u32[]{:S(2)}) copy-start(bf16[1,256,2304]{2,1,0:T(8,128)(2,1)} %param.18) | copy-start | bytes 3538948
  9.5 824.5 %all-reduce.5.cloned.1.call-start = ((), (), s32[]{:S(2)}) async-start(), calls=%async_computation.1 | async-start | bytes 294912 | tf_op jit(solution)/shard_map/psum | solution.py:34
  92.5 1054.2 %all-gather.5.cloned.1.call-start = ((), (), s32[]{:S(2)}) async-start(), calls=%async_computation.2 | async-start | bytes 3981312 | tf_op jit(solution)/shard_map/all_gather | solution.py:82
  834.0 17.3 %copy-start.4 = (f32[16,2304]{1,0:T(8,128)S(1)}, f32[16,2304]{1,0:T(8,128)}, u32[]{:S(2)}) copy-start(f32[16,2304]{1,0:T(8,128)} %all-reduce.5.cloned.1.call-done) | copy-start | bytes 442372
  851.3 1.1 copy-start.3
  851.8 206.6 %copy-start.2 = (s32[16,48,192]{2,1,0:T(8,128)S(1)}, s32[16,48,192]{2,1,0:T(8,128)}, u32[]{:S(2)}) copy-start(s32[16,48,192]{2,1,0:T(8,128)} %param.21) | copy-start | bytes 1769476
  1059.8 1.5 copy-start.5
Sparse Core Ops, SparseCore 0:
  10.3 82.1 all-reduce.2
  95.6 738.3 all-reduce.4
  1058.6 88.0 all-gather.4

commit v2 on v0

--- a/solution.py
+++ b/solution.py
@@ -79,7 +79,9 @@
         "rd,fd->rf", lowered_top, decoder[1], preferred_element_type=jnp.float32
     )
     tall_block = lax.all_gather(lowered_block, "feat", axis=0, tiled=True)
-    lowered_bottom = lax.all_gather(tall_block, "mp", axis=1, tiled=True)
+    lowered_bottom = jnp.concatenate(
+        lax.all_to_all(jnp.stack([tall_block] * lax.axis_size("mp")), "mp", 0, 0), axis=1
+    )
     bottom_scores = jnp.einsum(
         "rd,fd->rf", lowered_bottom, decoder[0], preferred_element_type=jnp.float32
     )

time: 761 us -> 806 us (1.059)
  the two profiles are of different devices: /device:TPU:2 before, /device:TPU:1 now
where the time goes in v2:
time: 806 us
  waiting for transfers between devices  529 us (66%)
  blocking collectives  209 us (26%)
  starting transfers between devices  32.5 us (4%)
  between operations  13.5 us (2%)
  matrix products  9.86 us (1%)
  local copies, waits for them, and re-layouts  8.86 us (1%)
    psum x1, waiting for transfers between devices, on_device(): lax.psum(jnp.dot(picker, unembed, preferred_element_type=jnp.float32), ('...  452 us
    all_gather x1, blocking collectives, on_device(): tall_block = lax.all_gather(lowered_block, 'feat', axis=0, tiled=True)  195 us
    all_to_all x1, waiting for transfers between devices, on_device(): lax.all_to_all(jnp.stack([tall_block] * lax.axis_size('mp')), 'mp', 0, 0)  76.1 us
    all_to_all x1, starting transfers between devices, on_device(): lax.all_to_all(jnp.stack([tall_block] * lax.axis_size('mp')), 'mp', 0, 0)  32.5 us
  transfers between devices with their start and end apart: 2, of which 2 were waited for; matrix products, arithmetic and copies ran while one was open for 1% of the time, Pallas kernels for 0%

profile of v2, /device:TPU:1, one launch (start us, length us, event | category | flops | bytes accessed | tf_op | source)
XLA Modules:
  0.0 805.6 jit_solution(8662714020569655093)
XLA Ops:
  6.5 0.0 copy-start
  6.5 0.0 copy-start.8
  6.5 0.0 copy-start.7
  6.5 0.0 all-reduce.2.cloned.1.call-start
  6.6 1.2 copy-done
  7.8 0.0 copy-start.1
  7.8 1.7 fusion.23
  9.5 0.0 all-reduce.2.cloned.1.call-update
  9.6 1.2 multiply_reduce_fusion
  10.8 1.2 divide_bitcast_fusion
  12.0 0.1 copy.23
  12.1 0.2 reshape.183
  12.3 0.1 constant_dynamic-slice_fusion
  12.4 0.1 copy.24
  12.4 0.0 copy-done.8
  12.5 0.1 fusion.27
  12.5 0.1 reshape.189
  12.6 0.0 copy-done.7
  12.6 0.1 reshape.182
  12.7 0.8 dynamic_slice.15
  13.5 0.1 dynamic-slice
  13.6 0.1 dynamic-slice_bitcast_fusion
  13.6 452.4 %all-reduce.2.cloned.1.call-done = f32[16,2304]{1,0:T(8,128)} async-done(((f32[16,2304]{1,0:T(8,128)}), f32[16,2304]{1,0:T(8,128)}) %all-reduce.2.cloned.1.call-update) | async-done | bytes 147472 | tf_op jit(solution)/shard_map/psum | solution.py:34
  466.0 0.0 copy-start.4
  466.0 2.9 fusion
  468.9 0.0 copy-done.1
  468.9 0.4 fusion.11
  469.3 13.9 %all-gather.1 = bf16[8,12,256]{2,1,0:T(8,128)(2,1)S(1)} all-gather(bf16[1,12,256]{2,1,0:T(8,128)(2,1)S(1)} %fusion.11), channel_id=2, replica_groups=mesh['mp'=8,'feat'=64] {'mp'}, dimensions={0}, use_global_device_ids=true | all-gather | bytes 55296 | tf_op jit(solution)/shard_map/all_gather | solution.py:66
  483.1 0.0 copy-done.4
  483.1 0.0 copy-start.3
  483.2 0.5 mul.102
  483.7 0.5 copy-done.3
  484.2 0.1 broadcast_in_dim.2
  484.3 0.4 fusion.7
  484.7 195.5 %all-gather.2 = bf16[64,12,288]{2,1,0:T(8,128)(2,1)S(1)} all-gather(bf16[1,12,288]{2,1,0:T(8,128)(2,1)S(1)} %fusion.7), channel_id=1, replica_groups=mesh['mp'=8,'feat'=64] {'feat'}, dimensions={0}, use_global_device_ids=true | all-gather | bytes 449280 | tf_op jit(solution)/shard_map/all_gather | solution.py:81
  680.2 0.3 reshape.194
  680.5 0.2 copy.25
  680.7 2.0 stack.2
  682.8 0.0 copy-start.2
  682.8 0.0 copy-start.6
  682.8 32.5 %all-to-all-start = ((bf16[8,768,288]{1,2,0:T(8,128)(2,1)}), bf16[8,768,288]{1,2,0:T(8,128)(2,1)}, u32[]{:S(2)}, u32[]{:S(2)}) async-start(bf16[8,768,288]{1,2,0:T(8,128)(2,1)} %stack.2), calls=%async_computation | async-start | bytes 7077888 | tf_op jit(solution)/shard_map/all_to_all | solution.py:83
  715.3 0.0 copy-done.2
  715.3 0.0 copy-done.6
  715.3 0.1 convert_multiply_fusion
  715.4 0.2 copy.26
  715.6 0.0 copy-start.5
  715.6 0.5 multiply_convert_fusion
  716.2 0.9 copy-done.5
  717.1 1.3 fusion.14
  718.4 76.1 %all-to-all-done = bf16[8,768,288]{1,2,0:T(8,128)(2,1)} async-done(((bf16[8,768,288]{1,2,0:T(8,128)(2,1)}), bf16[8,768,288]{1,2,0:T(8,128)(2,1)}, u32[]{:S(2)}, u32[]{:S(2)}) %all-to-all-start) | async-done | bytes 3538976 | tf_op jit(solution)/shard_map/all_to_all | solution.py:83
  794.5 3.1 fusion.1
  797.6 1.1 copy.27
  (4 shorter events, 0.0 us)
Async XLA Ops:
  6.5 1.3 copy-start
  6.5 5.9 copy-start.8
  6.5 6.1 copy-start.7
  6.5 459.5 %all-reduce.2.cloned.1.call-start = ((), (), s32[]{:S(2)}) async-start(), calls=%async_computation.1 | async-start | bytes 294912 | tf_op jit(solution)/shard_map/psum | solution.py:34
  7.8 461.1 %copy-start.1 = (bf16[1,256,2304]{2,1,0:T(8,128)(2,1)S(1)}, bf16[1,256,2304]{2,1,0:T(8,128)(2,1)}, u32[]{:S(2)}) copy-start(bf16[1,256,2304]{2,1,0:T(8,128)(2,1)} %param.18) | copy-start | bytes 3538948
  466.0 17.1 %copy-start.4 = (f32[16,2304]{1,0:T(8,128)S(1)}, f32[16,2304]{1,0:T(8,128)}, u32[]{:S(2)}) copy-start(f32[16,2304]{1,0:T(8,128)} %all-reduce.2.cloned.1.call-done) | copy-start | bytes 442372
  483.1 1.1 copy-start.3
  682.8 32.5 %copy-start.2 = (s32[16,48,192]{2,1,0:T(8,128)S(1)}, s32[16,48,192]{2,1,0:T(8,128)}, u32[]{:S(2)}) copy-start(s32[16,48,192]{2,1,0:T(8,128)} %param.21) | copy-start | bytes 1769476
  682.8 32.5 %copy-start.6 = (bf16[16,48,192]{2,1,0:T(8,128)(2,1)S(1)}, bf16[16,48,192]{2,1,0:T(8,128)(2,1)}, u32[]{:S(2)}) copy-start(bf16[16,48,192]{2,1,0:T(8,128)(2,1)} %param.20) | copy-start | bytes 884740
  682.8 111.7 %all-to-all-start = ((bf16[8,768,288]{1,2,0:T(8,128)(2,1)}), bf16[8,768,288]{1,2,0:T(8,128)(2,1)}, u32[]{:S(2)}, u32[]{:S(2)}) async-start(bf16[8,768,288]{1,2,0:T(8,128)(2,1)} %stack.2), calls=%async_computation | async-start | bytes 7077888 | tf_op jit(solution)/shard_map/all_to_all | solution.py:83
  715.6 1.5 copy-start.5
Sparse Core Ops, SparseCore 0:
  12.8 453.1 all-reduce.1
